TPU v7x, 256 devices: a whole 4x4x8 slice. The times are simulated.
256 devices in a mesh: dp: 8 (over x, core), expert: 32 (over z, y).
Axes of the slice: x: 4, y: 4, z: 8, core: 2. Of those that a mesh axis runs over, the one named last changes fastest.
Arguments:
- tokens: bfloat16 [4096, 2880], P(('dp', 'expert')), may hold values from -200 to 200
- norm_gain: float32 [2880], replicated, may hold values from 0.5 to 4
- router_weight: bfloat16 [2880, 32], replicated, may hold values from -0.02734375 to 0.02734375
- router_bias: float32 [32], replicated, may hold values from -1 to 1
- expert_ids: int32 [4096, 4], P(('dp', 'expert')), may hold values from 0 to 31, all different within a row; in each aligned block of 16 rows (0 to 15, 16 to 31, ...) at most 4 rows name the same one
- placement: int32 [32], replicated, may hold values from 0 to 31, each once
- gate_up: bfloat16 [32, 2, 2880, 2880], P('expert', None, None, 'dp'), may hold values from -0.109375 to 0.109375
- gate_up_bias: float32 [32, 2, 2880], P('expert', None, 'dp'), may hold values from -3 to 3
- down_proj: bfloat16 [32, 2880, 2880], P('expert', 'dp'), may hold values from -0.109375 to 0.109375
- down_bias: float32 [32, 2880], replicated, may hold values from -3 to 3
Outputs:
- mixed: bfloat16 [4096, 2880], P(('dp', 'expert'))
Inputs may be any that keep to these rules, and one draw needn't show every extreme that they name: `expert_ids`: in the rows of one device no expert is named more than 4 times; in every draw some device names some expert exactly 4 times. `placement`: every holder index appears once.
All inputs are finite; a program needn't handle non-finite values.
Results may differ from a plain program's by a relative error of at most 0.015.
Values may be sent and summed in bfloat16 or wider, within the bound.
A program may use at most 64 MiB of HBM per device.

v0:
```python
import jax
import jax.numpy as jnp
from jax import lax
from jax.sharding import PartitionSpec as P
from jax.experimental.layout import Layout, with_layout_constraint

TOPK = 4
EPS = 1e-05
LIMIT = 7.0
ALPHA = 1.702


def normalize(tokens, norm_gain):
    values = tokens.astype(jnp.float32)
    mean_square = jnp.mean(values * values, axis=-1, keepdims=True)
    return (values * lax.rsqrt(mean_square + EPS) * norm_gain).astype(jnp.bfloat16)


def routing(normed, router_weight, router_bias, expert_ids):
    logits = jnp.dot(normed, router_weight, preferred_element_type=jnp.float32) + router_bias
    expert_range = jnp.arange(logits.shape[1], dtype=jnp.int32)
    matches = expert_ids[:, :, None] == expert_range[None, None, :]
    picked = jnp.sum(jnp.where(matches, logits[:, None, :], 0.0), axis=2)
    powers = jnp.exp(picked)
    return powers / jnp.sum(powers, axis=1, keepdims=True)


def lookup(expert_ids, placement):
    return jnp.take(placement, expert_ids, mode="clip")


def slot_positions(columns, experts):
    flat_ids = columns.reshape(-1)
    order = jnp.arange(flat_ids.shape[0], dtype=jnp.int32)
    earlier = (flat_ids[:, None] == flat_ids[None, :]) & (order[None, :] < order[:, None])
    return jnp.sum(earlier.astype(jnp.int32), axis=1).reshape(columns.shape)


def swiglu(gate_value, up_value):
    gate_value = jnp.minimum(gate_value, LIMIT)
    up_value = jnp.clip(up_value, -LIMIT, LIMIT)
    return (up_value + 1.0) * gate_value * jax.nn.sigmoid(ALPHA * gate_value)


def body(
    tokens,
    norm_gain,
    router_weight,
    router_bias,
    expert_ids,
    placement,
    gate_up,
    gate_up_bias,
    down_proj,
    down_bias,
):
    tok_dev = tokens.shape[0]
    model_width = tokens.shape[1]
    experts = placement.shape[0]
    capacity = max(2, 2 * tok_dev * TOPK // experts)
    expert_count = lax.axis_size("expert")
    dp_count = lax.axis_size("dp")
    normed = normalize(tokens, norm_gain)
    weights = routing(normed, router_weight, router_bias, expert_ids)
    columns = lookup(expert_ids, placement)
    slots = slot_positions(columns, experts)
    target_row = columns * capacity + slots
    targets = jnp.arange(experts * capacity, dtype=jnp.int32)
    dispatch = jnp.sum(
        (target_row[:, :, None] == targets[None, None, :]).astype(jnp.int32), axis=1
    ).astype(jnp.bfloat16)
    outgoing = jnp.dot(dispatch.T, normed, preferred_element_type=jnp.float32).astype(jnp.bfloat16)
    outgoing = with_layout_constraint(outgoing, Layout(major_to_minor=(0, 1)))
    outgoing = outgoing.reshape(experts, capacity, model_width)
    gate_weight = gate_up[0, 0]
    up_weight = gate_up[0, 1]
    gate_bias = gate_up_bias[0, 0]
    up_bias = gate_up_bias[0, 1]
    down_weight = down_proj[0]
    group_width = gate_weight.shape[1]
    row_block = lax.all_to_all(outgoing, "expert", split_axis=0, concat_axis=0, tiled=True)
    row_block = row_block.reshape(experts * capacity, model_width)
    flat_rows = lax.all_gather(row_block, "dp", axis=0, tiled=True)
    gate_value = jnp.dot(flat_rows, gate_weight, preferred_element_type=jnp.float32) + gate_bias
    up_value = jnp.dot(flat_rows, up_weight, preferred_element_type=jnp.float32) + up_bias
    hidden = swiglu(gate_value, up_value).astype(jnp.bfloat16)
    hidden = hidden.reshape(dp_count, -1, hidden.shape[-1])
    partials = jnp.einsum("grf,fo->gro", hidden, down_weight, preferred_element_type=jnp.float32)
    partials = partials.astype(jnp.bfloat16)
    partials = with_layout_constraint(partials, Layout(major_to_minor=(0, 1, 2)))
    partials = partials.reshape(-1, model_width)
    reduced_parts = lax.psum_scatter(partials, "dp", scatter_dimension=0, tiled=True)
    reduced_parts = reduced_parts.reshape(expert_count, capacity, model_width)
    reduced = lax.all_to_all(reduced_parts, "expert", split_axis=0, concat_axis=0, tiled=True)
    reduced = reduced.reshape(experts, capacity, model_width)
    picked = reduced[columns.T, slots.T].astype(jnp.float32) + down_bias[columns.T]
    picked = picked.astype(jnp.bfloat16).astype(jnp.float32)
    return jnp.sum(weights.T[:, :, None] * picked, axis=0).astype(jnp.bfloat16)


def solution(mesh):
    return jax.shard_map(
        body,
        mesh=mesh,
        in_specs=(
            P(("dp", "expert"), None),
            P(),
            P(),
            P(),
            P(("dp", "expert"), None),
            P(),
            P("expert", None, None, "dp"),
            P("expert", None, "dp"),
            P("expert", "dp", None),
            P(),
        ),
        out_specs=P(("dp", "expert"), None),
        check_vma=False,
    )
```

profile of v0, /device:TPU:8, one launch (start us, length us, event | category | flops | bytes accessed | tf_op | source)
XLA Modules:
  0.0 188.9 jit_solution(12569673349516595402)
XLA Ops:
  6.5 0.9 copy.21
  7.5 0.1 reshape.52
  7.6 0.8 gather_fusion
  8.4 0.2 convert_reduce_fusion.1
  8.6 0.1 reshape.44
  8.9 0.1 fusion.15
  9.1 0.4 convolution_convert_fusion.1
  9.5 1.0 reshape.45
  10.5 33.6 %all_to_all.10 = bf16[32,4,2880]{2,1,0:T(4,128)(2,1)S(1)} all-to-all(bf16[32,4,2880]{2,1,0:T(4,128)(2,1)} %reshape.45), channel_id=1, replica_groups=mesh['dp'=8,'expert'=32] {'expert'}, dimensions={0} | all-to-all | bytes 1474560 | tf_op jit(solution)/shard_map/all_to_all | solution.py:81
  44.1 1.2 reshape.46
  45.5 39.1 %all-gather.2.cloned.1.call-done = bf16[1024,2880]{1,0:T(8,128)(2,1)} async-done(((bf16[128,2880]{1,0:T(8,128)(2,1)}), bf16[1024,2880]{1,0:T(8,128)(2,1)}) %all-gather.2.cloned.1.call-update) | async-done | bytes 5898256 | tf_op jit(solution)/shard_map/all_gather | solution.py:83
  84.6 6.0 %fusion.1 = f32[1024,360]{0,1:T(8,128)S(1)} fusion(bf16[1024,2880]{1,0:T(8,128)(2,1)} %all-gather.2.cloned.1.call-done, bf16[1,2,2880,360]{2,3,1,0:T(8,128)(2,1)} %param.16), kind=kOutput, calls=%fused_computation.6 | convolution fusion | flops 2123366400 | bytes 9623552 | tf_op jit(solution)/shard_map/dot_general | solution.py:84
  90.5 4.4 %fusion.9 = bf16[45,8,8,128]{3,2,1,0:T(8,128)(2,1)S(1)} fusion(f32[1024,360]{0,1:T(8,128)S(1)} %fusion.1, bf16[1024,2880]{1,0:T(8,128)(2,1)S(1)} %copy-done.7, bf16[1,2,2880,360]{2,3,1,0:T(8,128)(2,1)} %param.16, f32[360]{0:T(512)S(1)} %get-tuple-element.6, f32[360]{0:T(512)S(1)} %get-tuple-element.5), kind=kOutput, calls=%fused_computation.13 | convolution fusion | flops 2127790080 | bytes 10232640 | tf_op jit(solution)/shard_map/dot_general | solution.py:85
  95.0 5.4 %convolution_convert_fusion = bf16[8,128,2880]{2,1,0:T(8,128)(2,1)} fusion(bf16[1,360,2880]{2,1,0:T(8,128)(2,1)S(1)} %copy-done, bf16[45,8,8,128]{3,2,1,0:T(8,128)(2,1)S(1)} %fusion.9), kind=kOutput, calls=%fused_computation.3 | convolution fusion | flops 2126315520 | bytes 8709120 | tf_op jit(solution)/shard_map/grf,fo->gro/dot_general | solution.py:88
  100.5 44.3 %reduce-scatter.2.cloned.1.call-done = bf16[128,2880]{1,0:T(8,128)(2,1)} async-done(((bf16[1024,2880]{1,0:T(8,128)(2,1)}), bf16[128,2880]{1,0:T(8,128)(2,1)}) %reduce-scatter.2.cloned.1.call-update) | async-done | bytes 737296 | tf_op jit(solution)/shard_map/reduce_scatter | solution.py:92
  144.8 2.4 %reshape.49 = bf16[32,4,2880]{2,1,0:T(4,128)(2,1)} reshape(bf16[128,2880]{1,0:T(8,128)(2,1)} %reduce-scatter.2.cloned.1.call-done) | data formatting | bytes 1474560 | tf_op jit(solution)/shard_map/reshape | solution.py:93
  147.1 10.3 %all-to-all-start.1 = ((bf16[32,4,2880]{2,1,0:T(4,128)(2,1)}), bf16[32,4,2880]{2,1,0:T(4,128)(2,1)S(1)}, u32[]{:S(2)}, u32[]{:S(2)}) async-start(bf16[32,4,2880]{2,1,0:T(4,128)(2,1)} %reshape.49), calls=%async_computation.2 | async-start | bytes 1507328 | tf_op jit(solution)/shard_map/all_to_all | solution.py:94
  157.9 1.7 gather_fusion.2
  159.6 1.1 convolution_add_fusion
  160.7 0.2 select_reduce_fusion
  160.9 17.3 %all-to-all-done.1 = bf16[32,4,2880]{2,1,0:T(4,128)(2,1)S(1)} async-done(((bf16[32,4,2880]{2,1,0:T(4,128)(2,1)}), bf16[32,4,2880]{2,1,0:T(4,128)(2,1)S(1)}, u32[]{:S(2)}, u32[]{:S(2)}) %all-to-all-start.1) | async-done | bytes 737312 | tf_op jit(solution)/shard_map/all_to_all | solution.py:94
  178.2 1.8 gather_fusion.1
  180.1 1.2 add_convert_fusion
  181.3 0.8 fusion.12
  (37 shorter events, 0.8 us)
Async XLA Ops:
  6.5 88.5 %copy-start = (bf16[1,360,2880]{2,1,0:T(8,128)(2,1)S(1)}, bf16[1,360,2880]{2,1,0:T(8,128)(2,1)}, u32[]{:S(2)}) copy-start(bf16[1,360,2880]{2,1,0:T(8,128)(2,1)} %param.18) | copy-start | bytes 6220804
  6.5 1.0 copy-start.1
  6.5 78.0 %all-gather.2.cloned.1.call-start = ((), (), s32[]{:S(2)}) async-start(), calls=%async_computation.3 | async-start | bytes 6782976 | tf_op jit(solution)/shard_map/all_gather | solution.py:83
  7.6 1.3 copy-start.3
  7.6 1.5 copy-start.4
  10.5 34.9 %copy-start.6 = (f32[1,2,360]{2,1,0:T(2,128)S(1)}, f32[1,2,360]{2,1,0:T(2,128)}, u32[]{:S(2)}) copy-start(f32[1,2,360]{2,1,0:T(2,128)} %param.17) | copy-start | bytes 8644
  45.4 99.4 %reduce-scatter.2.cloned.1.call-start = ((), (), s32[]{:S(2)}) async-start(), calls=%async_computation.4 | async-start | bytes 6782976 | tf_op jit(solution)/shard_map/reduce_scatter | solution.py:92
  84.5 6.0 %copy-start.7 = (bf16[1024,2880]{1,0:T(8,128)(2,1)S(1)}, bf16[1024,2880]{1,0:T(8,128)(2,1)}, u32[]{:S(2)}) copy-start(bf16[1024,2880]{1,0:T(8,128)(2,1)} %all-gather.2.cloned.1.call-done) | copy-start | bytes 17694724
  100.5 57.4 %copy-start.2 = (f32[32,2880]{1,0:T(8,128)S(1)}, f32[32,2880]{1,0:T(8,128)}, u32[]{:S(2)}) copy-start(f32[32,2880]{1,0:T(8,128)} %param.19) | copy-start | bytes 1105924
  147.1 31.1 %all-to-all-start.1 = ((bf16[32,4,2880]{2,1,0:T(4,128)(2,1)}), bf16[32,4,2880]{2,1,0:T(4,128)(2,1)S(1)}, u32[]{:S(2)}, u32[]{:S(2)}) async-start(bf16[32,4,2880]{2,1,0:T(4,128)(2,1)} %reshape.49), calls=%async_computation.2 | async-start | bytes 1507328 | tf_op jit(solution)/shard_map/all_to_all | solution.py:94
  157.8 1.7 copy-start.8
  157.8 2.9 %copy-start.5 = (s32[16,4]{0,1:T(4,128)S(1)}, s32[16,4]{0,1:T(4,128)}, u32[]{:S(2)}) copy-start(s32[16,4]{0,1:T(4,128)} %param.14) | copy-start | bytes 772
Sparse Core Ops, SparseCore 0:
  45.5 39.0 all-gather.1
  100.6 44.1 reduce-scatter.1
where the time goes:
time: 189 us
  waiting for transfers between devices  101 us (53%)
  blocking collectives  33.6 us (18%)
  matrix products  17.4 us (9%)
  between operations  13.6 us (7%)
  local copies, waits for them, and re-layouts  10.6 us (6%)
  starting transfers between devices  10.4 us (6%)
  other arithmetic  2.61 us (1%)
    reduce_scatter x1, waiting for transfers between devices, body(): lax.psum_scatter(partials, 'dp', scatter_dimension=0, tiled=True)  44.3 us
    all_gather x1, waiting for transfers between devices, body(): flat_rows = lax.all_gather(row_block, 'dp', axis=0, tiled=True)  39.1 us
    all_to_all x1, blocking collectives, body(): lax.all_to_all(outgoing, 'expert', split_axis=0, concat_axis=0, tiled=True)  33.6 us
    all_to_all x1, waiting for transfers between devices, body(): lax.all_to_all(reduced_parts, 'expert', split_axis=0, concat_axis=0, tile...  17.3 us
    all_to_all x1, starting transfers between devices, body(): lax.all_to_all(reduced_parts, 'expert', split_axis=0, concat_axis=0, tile...  10.3 us
    dot_general x1, matrix products, body(): jnp.dot(flat_rows, gate_weight, preferred_element_type=jnp.float32)  5.98 us
    dot_general x1, matrix products, body(): jnp.einsum('grf,fo->gro', hidden, down_weight, preferred_element_type=jnp...  5.42 us
    dot_general x1, matrix products, body(): jnp.dot(flat_rows, up_weight, preferred_element_type=jnp.float32) + up_bias  4.45 us
  transfers between devices with their start and end apart: 3, of which 3 were waited for; matrix products, arithmetic and copies ran while one was open for 2% of the time, Pallas kernels for 0%

commit v1 on v0

--- a/solution.py
+++ b/solution.py
@@ -80,7 +80,9 @@
     group_width = gate_weight.shape[1]
     row_block = lax.all_to_all(outgoing, "expert", split_axis=0, concat_axis=0, tiled=True)
     row_block = row_block.reshape(experts * capacity, model_width)
-    flat_rows = lax.all_gather(row_block, "dp", axis=0, tiled=True)
+    flat_rows = jnp.concatenate(
+        lax.all_to_all(jnp.stack([row_block] * lax.axis_size("dp")), "dp", 0, 0), axis=0
+    )
     gate_value = jnp.dot(flat_rows, gate_weight, preferred_element_type=jnp.float32) + gate_bias
     up_value = jnp.dot(flat_rows, up_weight, preferred_element_type=jnp.float32) + up_bias
     hidden = swiglu(gate_value, up_value).astype(jnp.bfloat16)

time: 189 us -> 230 us (1.22)
  waiting for transfers between devices: 101 us -> 124 us
  local copies, waits for them, and re-layouts: 10.6 us -> 24.1 us
  starting transfers between devices: 10.4 us -> 15 us
    all_to_all x0 -> x1, waiting for transfers between devices: none -> 67.8 us  [body(): lax.all_to_all(jnp.stack([row_block] * lax.axis_size('dp')), 'dp', 0, 0)]
    all_gather x1 -> x0, waiting for transfers between devices: 39.1 us -> none  [body(): flat_rows = lax.all_gather(row_block, 'dp', axis=0, tiled=True)]
    all_to_all x0 -> x1, local copies, waits for them, and re-layouts: none -> 8.45 us  [body(): lax.all_to_all(jnp.stack([row_block] * lax.axis_size('dp')), 'dp', 0, 0)]
    another operation x0 -> x3, local copies, waits for them, and re-layouts: none -> 6 us  [body(): jnp.stack([row_block] * lax.axis_size('dp'))]
    reduce_scatter x1, waiting for transfers between devices: 44.3 us -> 39.1 us  [body(): lax.psum_scatter(partials, 'dp', scatter_dimension=0, tiled=True)]
    all_to_all x0 -> x1, starting transfers between devices: none -> 4.85 us  [body(): lax.all_to_all(jnp.stack([row_block] * lax.axis_size('dp')), 'dp', 0, 0)]
  transfers between devices with their start and end apart: 3 -> 3, of which waited for: 3 -> 3; matrix products, arithmetic and copies ran while one was open for 2% -> 1% of each run, Pallas kernels for 0% -> 0%
where the time goes in v1:
time: 230 us; the launch traced here: 229 us
  waiting for transfers between devices  124 us (54%)
  blocking collectives  33.4 us (15%)
  local copies, waits for them, and re-layouts  24.1 us (10%)
  matrix products  15.8 us (7%)
  starting transfers between devices  15 us (7%)
  between operations  13.6 us (6%)
  other arithmetic  2.61 us (1%)
    all_to_all x1, waiting for transfers between devices, body(): lax.all_to_all(jnp.stack([row_block] * lax.axis_size('dp')), 'dp', 0, 0)  67.8 us
    reduce_scatter x1, waiting for transfers between devices, body(): lax.psum_scatter(partials, 'dp', scatter_dimension=0, tiled=True)  39.1 us
    all_to_all x1, blocking collectives, body(): lax.all_to_all(outgoing, 'expert', split_axis=0, concat_axis=0, tiled=True)  33.4 us
    all_to_all x1, waiting for transfers between devices, body(): lax.all_to_all(reduced_parts, 'expert', split_axis=0, concat_axis=0, tile...  17.5 us
    all_to_all x1, starting transfers between devices, body(): lax.all_to_all(reduced_parts, 'expert', split_axis=0, concat_axis=0, tile...  10.1 us
    all_to_all x1, local copies, waits for them, and re-layouts, body(): lax.all_to_all(jnp.stack([row_block] * lax.axis_size('dp')), 'dp', 0, 0)  8.45 us
    another operation x3, local copies, waits for them, and re-layouts, body(): jnp.stack([row_block] * lax.axis_size('dp'))  6 us
    dot_general x1, matrix products, body(): jnp.dot(flat_rows, gate_weight, preferred_element_type=jnp.float32)  5.98 us
  transfers between devices with their start and end apart: 3, of which 3 were waited for; matrix products, arithmetic and copies ran while one was open for 1% of the time, Pallas kernels for 0%

profile of v1, /device:TPU:8, one launch (start us, length us, event | category | flops | bytes accessed | tf_op | source)
XLA Modules:
  0.0 229.0 jit_solution(13551698982978328477)
XLA Ops:
  6.5 0.9 copy.34
  7.6 0.8 gather_fusion
  9.1 0.4 convolution_convert_fusion.1
  9.5 1.0 reshape.47
  10.5 33.4 %all_to_all.15 = bf16[32,4,2880]{2,1,0:T(4,128)(2,1)S(1)} all-to-all(bf16[32,4,2880]{2,1,0:T(4,128)(2,1)} %reshape.47), channel_id=1, replica_groups=mesh['dp'=8,'expert'=32] {'expert'}, dimensions={0} | all-to-all | bytes 1474560 | tf_op jit(solution)/shard_map/all_to_all | solution.py:81
  44.0 1.2 stack_reshape.2
  45.2 1.5 copy.36
  46.7 3.3 %stack.3 = bf16[8,128,2880]{1,2,0:T(8,128)(2,1)} broadcast(bf16[128,2880]{0,1:T(8,128)(2,1)S(1)} %copy.36), dimensions={1,2} | broadcast | bytes 6635520 | tf_op jit(solution)/shard_map/stack | solution.py:84
  50.0 4.8 %all-to-all-start.1 = ((bf16[8,128,2880]{1,2,0:T(8,128)(2,1)}), bf16[8,128,2880]{1,2,0:T(8,128)(2,1)}, u32[]{:S(2)}, u32[]{:S(2)}) async-start(bf16[8,128,2880]{1,2,0:T(8,128)(2,1)} %stack.3), calls=%async_computation.1 | async-start | bytes 11796480 | tf_op jit(solution)/shard_map/all_to_all | solution.py:84
  54.9 67.8 %all-to-all-done.1 = bf16[8,128,2880]{1,2,0:T(8,128)(2,1)} async-done(((bf16[8,128,2880]{1,2,0:T(8,128)(2,1)}), bf16[8,128,2880]{1,2,0:T(8,128)(2,1)}, u32[]{:S(2)}, u32[]{:S(2)}) %all-to-all-start.1) | async-done | bytes 5898272 | tf_op jit(solution)/shard_map/all_to_all | solution.py:84
  122.7 8.4 %copy.37 = bf16[8,128,2880]{2,1,0:T(8,128)(2,1)} copy(bf16[8,128,2880]{1,2,0:T(8,128)(2,1)} %all-to-all-done.1) | data formatting | bytes 11796480 | tf_op jit(solution)/shard_map/all_to_all | solution.py:84
  131.2 6.0 %fusion.1 = f32[1024,360]{0,1:T(8,128)S(1)} fusion(bf16[1024,2880]{1,0:T(8,128)(2,1)} %bitcast.35, bf16[1,2,2880,360]{2,3,1,0:T(8,128)(2,1)} %param.16), kind=kOutput, calls=%fused_computation.6 | convolution fusion | flops 2123366400 | bytes 9623552 | tf_op jit(solution)/shard_map/dot_general | solution.py:86
  137.2 0.3 slice-done.1
  137.5 2.9 %fusion.9 = bf16[45,8,8,128]{3,2,1,0:T(8,128)(2,1)S(1)} fusion(f32[1024,360]{0,1:T(8,128)S(1)} %fusion.1, bf16[1024,2880]{1,0:T(8,128)(2,1)S(1)} %bitcast.36, bf16[1,2,2880,360]{2,3,1,0:T(8,128)(2,1)S(1)} %bitcast.39, f32[360]{0:T(512)S(1)} %get-tuple-element.6, f32[360]{0:T(512)S(1)} %get-tuple-element.5), kind=kOutput, calls=%fused_computation.13 | convolution fusion | flops 2127790080 | bytes 10364928 | tf_op jit(solution)/shard_map/dot_general | solution.py:87
  140.4 5.4 %convolution_convert_fusion = bf16[8,128,2880]{2,1,0:T(8,128)(2,1)} fusion(bf16[1,360,2880]{2,1,0:T(8,128)(2,1)S(1)} %copy-done, bf16[45,8,8,128]{3,2,1,0:T(8,128)(2,1)S(1)} %fusion.9), kind=kOutput, calls=%fused_computation.3 | convolution fusion | flops 2126315520 | bytes 8709120 | tf_op jit(solution)/shard_map/grf,fo->gro/dot_general | solution.py:90
  145.8 39.1 %reduce-scatter.2.cloned.1.call-done = bf16[128,2880]{1,0:T(8,128)(2,1)} async-done(((bf16[1024,2880]{1,0:T(8,128)(2,1)}), bf16[128,2880]{1,0:T(8,128)(2,1)}) %reduce-scatter.2.cloned.1.call-update) | async-done | bytes 737296 | tf_op jit(solution)/shard_map/reduce_scatter | solution.py:94
  185.0 2.4 %reshape.51 = bf16[32,4,2880]{2,1,0:T(4,128)(2,1)} reshape(bf16[128,2880]{1,0:T(8,128)(2,1)} %reduce-scatter.2.cloned.1.call-done) | data formatting | bytes 1474560 | tf_op jit(solution)/shard_map/reshape | solution.py:95
  187.3 10.1 %all-to-all-start.2 = ((bf16[32,4,2880]{2,1,0:T(4,128)(2,1)}), bf16[32,4,2880]{2,1,0:T(4,128)(2,1)S(1)}, u32[]{:S(2)}, u32[]{:S(2)}) async-start(bf16[32,4,2880]{2,1,0:T(4,128)(2,1)} %reshape.51), calls=%async_computation.3 | async-start | bytes 1507328 | tf_op jit(solution)/shard_map/all_to_all | solution.py:96
  197.8 1.7 gather_fusion.2
  199.5 1.1 convolution_add_fusion
  200.9 17.5 %all-to-all-done.2 = bf16[32,4,2880]{2,1,0:T(4,128)(2,1)S(1)} async-done(((bf16[32,4,2880]{2,1,0:T(4,128)(2,1)}), bf16[32,4,2880]{2,1,0:T(4,128)(2,1)S(1)}, u32[]{:S(2)}, u32[]{:S(2)}) %all-to-all-start.2) | async-done | bytes 737312 | tf_op jit(solution)/shard_map/all_to_all | solution.py:96
  218.4 1.8 gather_fusion.1
  220.2 1.2 add_convert_fusion
  221.4 0.8 fusion.12
  (44 shorter events, 1.4 us)
Async XLA Ops:
  6.5 133.8 %copy-start = (bf16[1,360,2880]{2,1,0:T(8,128)(2,1)S(1)}, bf16[1,360,2880]{2,1,0:T(8,128)(2,1)}, u32[]{:S(2)}) copy-start(bf16[1,360,2880]{2,1,0:T(8,128)(2,1)} %param.18) | copy-start | bytes 6220804
  6.5 1.0 copy-start.1
  7.6 1.3 copy-start.4
  7.6 1.5 copy-start.5
  50.0 4.9 %copy-start.7 = (f32[1,2,360]{2,1,0:T(2,128)S(1)}, f32[1,2,360]{2,1,0:T(2,128)}, u32[]{:S(2)}) copy-start(f32[1,2,360]{2,1,0:T(2,128)} %param.17) | copy-start | bytes 8644
  50.0 72.8 %all-to-all-start.1 = ((bf16[8,128,2880]{1,2,0:T(8,128)(2,1)}), bf16[8,128,2880]{1,2,0:T(8,128)(2,1)}, u32[]{:S(2)}, u32[]{:S(2)}) async-start(bf16[8,128,2880]{1,2,0:T(8,128)(2,1)} %stack.3), calls=%async_computation.1 | async-start | bytes 11796480 | tf_op jit(solution)/shard_map/all_to_all | solution.py:84
  54.8 130.1 %reduce-scatter.2.cloned.1.call-start = ((), (), s32[]{:S(2)}) async-start(), calls=%async_computation.4 | async-start | bytes 6782976 | tf_op jit(solution)/shard_map/reduce_scatter | solution.py:94
  122.7 14.4 %slice-start = ((s8[4239360]{0:T(1024)(128)(4,1)}), s8[45056]{0:T(1024)(128)(4,1)S(1)}, s32[]{:S(2)}) async-start(s8[4239360]{0:T(1024)(128)(4,1)} %bitcast.38), calls=%async_computation.5 | async-start | bytes 90112
  131.2 6.0 %copy-start.3 = (bf16[8,128,2880]{2,1,0:T(8,128)(2,1)S(1)}, bf16[8,128,2880]{2,1,0:T(8,128)(2,1)}, u32[]{:S(2)}) copy-start(bf16[8,128,2880]{2,1,0:T(8,128)(2,1)} %copy.37) | copy-start | bytes 17694724
  131.2 6.3 %slice-start.1 = ((s8[4239360]{0:T(1024)(128)(4,1)}), s8[4194304]{0:T(1024)(128)(4,1)S(1)}, s32[]{:S(2)}) async-start(s8[4239360]{0:T(1024)(128)(4,1)} %bitcast.38), calls=%async_computation.6 | async-start | bytes 8388608
  145.8 52.0 %copy-start.2 = (f32[32,2880]{1,0:T(8,128)S(1)}, f32[32,2880]{1,0:T(8,128)}, u32[]{:S(2)}) copy-start(f32[32,2880]{1,0:T(8,128)} %param.19) | copy-start | bytes 1105924
  187.3 31.1 %all-to-all-start.2 = ((bf16[32,4,2880]{2,1,0:T(4,128)(2,1)}), bf16[32,4,2880]{2,1,0:T(4,128)(2,1)S(1)}, u32[]{:S(2)}, u32[]{:S(2)}) async-start(bf16[32,4,2880]{2,1,0:T(4,128)(2,1)} %reshape.51), calls=%async_computation.3 | async-start | bytes 1507328 | tf_op jit(solution)/shard_map/all_to_all | solution.py:96
  197.8 1.7 copy-start.8
  197.8 2.9 %copy-start.6 = (s32[16,4]{0,1:T(4,128)S(1)}, s32[16,4]{0,1:T(4,128)}, u32[]{:S(2)}) copy-start(s32[16,4]{0,1:T(4,128)} %param.14) | copy-start | bytes 772
Sparse Core Ops, SparseCore 0:
  145.9 38.9 reduce-scatter.1
